TPU v7x, 32 devices: a whole 2x2x4 slice. The times are simulated.
32 devices in a mesh: slab: 8 (over z, x), head: 4 (over y, core).
Axes of the slice: x: 2, y: 2, z: 4, core: 2. Of those that a mesh axis runs over, the one named last changes fastest.
Arguments:
- atom_feats: bfloat16 [2, 4096, 128], P(None, 'slab'), may hold values from -16 to 16
- pair_feats: bfloat16 [4096, 16, 128], P('slab'), may hold values from -8 to 330
- tok_slot: int32 [4096], P('slab'), may hold values from 0 to 255, as said below
- w_proj: bfloat16 [4, 128, 128], P(None, None, 'head'), may hold values from -0.5 to 0.5
- w_out: bfloat16 [128, 128], P('head'), may hold values from -0.5 to 0.5
- w_pair: bfloat16 [16, 4], P(None, 'head'), may hold values from -1.2 to 1.2
- w_tok: bfloat16 [128, 768], P(None, 'head'), may hold values from -0.5 to 0.5
- d_tok: bfloat16 [2, 256, 768], P(None, 'slab', 'head'), may hold values from -6 to 6
Outputs:
- tok_act: bfloat16 [2, 256, 768], P(None, 'slab', 'head')
- grad_proj: float32 [4, 128, 128], P(None, None, 'head')
- grad_out: float32 [128, 128], P('head')
- grad_pair: float32 [16, 4], P(None, 'head')
- grad_tok: float32 [128, 768], P(None, 'head')
Inputs may be any that keep to these rules, and one draw needn't show every extreme that they name: `tok_slot`: never falling. The atoms s * 512 to (s + 1) * 512 - 1 use slots s * 32 to s * 32 + n - 1, each at least once, with n from 16 to 32; the first of these atoms is in slot s * 32. The last slab and one other use all 32 slots.
All inputs are finite; a program needn't handle non-finite values.
Results may differ from a plain program's by a relative error of at most 0.023.
Values may be sent and summed in bfloat16 or wider, within the bound.
A program may use at most 64 MiB of HBM per device.

v0:
```python
import jax
import jax.numpy as jnp
from jax import lax
from jax.sharding import PartitionSpec as P

Q_WIN = 32
K_WIN = 128
RIM = 48
EPSILON = 1e-05


def extended_2(cells, sides, width):
    for axis, dim in sides:
        count = lax.axis_size(axis)
        ends = count - 1
        head = lax.slice_in_dim(cells, 0, width, axis=dim)
        tail = lax.slice_in_dim(cells, cells.shape[dim] - width, cells.shape[dim], axis=dim)
        cells = jnp.concatenate(
            [
                lax.ppermute(tail, axis, [(i, (i + 1) % count) for i in range(ends)]),
                cells,
                lax.ppermute(head, axis, [((i + 1) % count, i) for i in range(ends)]),
            ],
            axis=dim,
        )
    return cells


def key_windows(extended, block_count):
    leading = extended.shape[:-2]
    last_width = extended.shape[-1]
    row_total = block_count * Q_WIN
    pieces = []
    for offset in range(K_WIN // Q_WIN):
        segment = lax.slice_in_dim(
            extended, Q_WIN * offset, Q_WIN * offset + row_total, axis=extended.ndim - 2
        )
        pieces.append(segment.reshape(leading + (block_count, Q_WIN, last_width)))
    return jnp.concatenate(pieces, axis=-2)


def key_unwindowed_rows(windowed, block_count):
    leading = windowed.shape[:-3]
    last_width = windowed.shape[-1]
    row_total = block_count * Q_WIN
    margin = K_WIN - Q_WIN
    summed = None
    for offset in range(K_WIN // Q_WIN):
        segment = windowed[..., Q_WIN * offset : Q_WIN * (offset + 1), :].reshape(
            leading + (row_total, last_width)
        )
        padding = [(0, 0)] * len(leading) + [(Q_WIN * offset, margin - Q_WIN * offset), (0, 0)]
        segment = jnp.pad(segment, padding)
        summed = segment if summed is None else summed + segment
    return summed


def on_device(atom_feats, pair_feats, tok_slot, w_proj, w_out, w_pair, w_tok, d_tok):
    samples, atom_count, feature_width = atom_feats.shape
    head_width = w_proj.shape[2]
    block_count = atom_count // Q_WIN
    slot_count = d_tok.shape[1]
    slab_index = lax.axis_index("slab")
    slab_total = lax.axis_size("slab")
    score_scale = head_width ** (-0.5)
    feats_float = atom_feats.astype(jnp.float32)
    centered = feats_float - jnp.mean(feats_float, axis=2, keepdims=True)
    variance = jnp.mean(centered * centered, axis=2, keepdims=True)
    normed = (centered * lax.rsqrt(variance + EPSILON)).astype(jnp.bfloat16)
    projected = jnp.einsum("saw,fwd->fsad", normed, w_proj, preferred_element_type=jnp.float32)
    queries = (projected[0] * score_scale).astype(jnp.bfloat16)
    keys_local = projected[1].astype(jnp.bfloat16)
    values_local = projected[2].astype(jnp.bfloat16)
    gating = jax.nn.sigmoid(projected[3])
    stacked = jnp.stack([keys_local, values_local])
    extended = extended_2(stacked, (("slab", 2),), RIM)
    windowed = key_windows(extended, block_count)
    key_window_rows = windowed[0]
    value_window_rows = windowed[1]
    query_block_rows = queries.reshape(samples, block_count, Q_WIN, head_width)
    pair_bias_terms = jnp.einsum(
        "acj,c->aj", pair_feats, w_pair[:, 0], preferred_element_type=jnp.float32
    )
    pair_bias_terms = pair_bias_terms.reshape(block_count, Q_WIN, K_WIN)
    positions = (
        slab_index * atom_count
        + Q_WIN * jnp.arange(block_count, dtype=jnp.int32)[:, None]
        - RIM
        + jnp.arange(K_WIN, dtype=jnp.int32)[None, :]
    )
    in_range = (positions >= 0) & (positions < atom_count * slab_total)
    attention_scores = (
        jnp.einsum(
            "sbqd,sbkd->sbqk", query_block_rows, key_window_rows, preferred_element_type=jnp.float32
        )
        + pair_bias_terms[None]
    )
    attention_scores = jnp.where(in_range[None, :, None, :], attention_scores, -jnp.inf)
    highest = jnp.max(attention_scores, axis=3, keepdims=True)
    exponent = jnp.exp(attention_scores - highest)
    attn_weights = exponent / jnp.sum(exponent, axis=3, keepdims=True)
    weight_half_precision = attn_weights.astype(jnp.bfloat16)
    attended_output = jnp.einsum(
        "sbqk,sbkd->sbqd",
        weight_half_precision,
        value_window_rows,
        preferred_element_type=jnp.float32,
    )
    attended_output = attended_output.reshape(samples, atom_count, head_width)
    heads_out = (gating * attended_output).astype(jnp.bfloat16)
    head_part = jnp.einsum(
        "nsad,ndw->nsaw",
        lax.all_gather(heads_out[None], "head", axis=0, tiled=True),
        lax.all_gather(w_out[None], "head", axis=0, tiled=True),
        preferred_element_type=jnp.float32,
    )
    rounded = lax.optimization_barrier(head_part.astype(jnp.bfloat16)).astype(jnp.float32)
    attn_sum = jnp.sum(rounded, axis=0)
    mixed_half = (feats_float + attn_sum).astype(jnp.bfloat16)
    pre_act = jnp.einsum("saw,wh->sah", mixed_half, w_tok, preferred_element_type=jnp.float32)
    act_gate = jax.nn.sigmoid(pre_act)
    atom_act = (pre_act * act_gate).astype(jnp.bfloat16)
    own_slots = slab_index * slot_count + jnp.arange(slot_count, dtype=jnp.int32)
    member = (tok_slot[:, None] == own_slots[None, :]).astype(jnp.bfloat16)
    counts = jnp.sum(member, axis=0, dtype=jnp.float32)
    divisor = jnp.maximum(counts, 1.0)
    token_sums = jnp.einsum("at,sah->sth", member, atom_act, preferred_element_type=jnp.float32)
    tok_act = (token_sums / divisor[None, :, None]).astype(jnp.bfloat16)
    tok_grad = (d_tok.astype(jnp.float32) / divisor[None, :, None]).astype(jnp.bfloat16)
    spread = jnp.einsum("at,sth->sah", member, tok_grad, preferred_element_type=jnp.float32)
    slope = act_gate * (1.0 + pre_act * (1.0 - act_gate))
    act_grad = (spread * slope).astype(jnp.bfloat16)
    grad_tok_local = jnp.einsum(
        "saw,sah->wh", mixed_half, act_grad, preferred_element_type=jnp.float32
    )
    mixed_terms = jnp.einsum("sah,wh->saw", act_grad, w_tok, preferred_element_type=jnp.float32)
    mixed_grad = lax.psum(mixed_terms.astype(jnp.bfloat16), "head")
    out_grad = jnp.einsum("saw,dw->sad", mixed_grad, w_out, preferred_element_type=jnp.float32)
    grad_out_local = jnp.einsum(
        "sad,saw->dw", heads_out, mixed_grad, preferred_element_type=jnp.float32
    )
    att_grad = (gating * out_grad).astype(jnp.bfloat16)
    gate_grad = (out_grad * attended_output * gating * (1.0 - gating)).astype(jnp.bfloat16)
    attention_block_rows = att_grad.reshape(samples, block_count, Q_WIN, head_width)
    probability_gradient = jnp.einsum(
        "sbqd,sbkd->sbqk",
        attention_block_rows,
        value_window_rows,
        preferred_element_type=jnp.float32,
    )
    score_grad = (
        attn_weights
        * (
            probability_gradient
            - jnp.sum(attn_weights * probability_gradient, axis=3, keepdims=True)
        )
    ).astype(jnp.bfloat16)
    query_gradient = score_scale * jnp.einsum(
        "sbqk,sbkd->sbqd", score_grad, key_window_rows, preferred_element_type=jnp.float32
    )
    query_gradient = query_gradient.reshape(samples, atom_count, head_width).astype(jnp.bfloat16)
    key_win_grad = jnp.einsum(
        "sbqk,sbqd->sbkd", score_grad, query_block_rows, preferred_element_type=jnp.float32
    )
    value_win_grad = jnp.einsum(
        "sbqk,sbqd->sbkd",
        weight_half_precision,
        attention_block_rows,
        preferred_element_type=jnp.float32,
    )
    spilled = key_unwindowed_rows(jnp.stack([key_win_grad, value_win_grad]), block_count)
    rim_local = jnp.concatenate([spilled[:, :, :RIM], spilled[:, :, RIM + atom_count :]], axis=2)
    returned = extended_2(rim_local.astype(jnp.bfloat16), (("slab", 2),), RIM).astype(
        rim_local.dtype
    )
    from_before = returned[:, :, :RIM]
    from_after = returned[:, :, 3 * RIM :]
    own_part = spilled[:, :, RIM : RIM + atom_count]
    own_part = own_part + jnp.pad(from_before, ((0, 0), (0, 0), (0, atom_count - RIM), (0, 0)))
    own_part = own_part + jnp.pad(from_after, ((0, 0), (0, 0), (atom_count - RIM, 0), (0, 0)))
    kv_grad = own_part.astype(jnp.bfloat16)
    grads_stack = jnp.stack([query_gradient, kv_grad[0], kv_grad[1], gate_grad])
    grad_proj_local = jnp.einsum(
        "saw,fsad->fwd", normed, grads_stack, preferred_element_type=jnp.float32
    )
    bias_grad = (
        jnp.sum(score_grad, axis=0, dtype=jnp.float32)
        .astype(jnp.bfloat16)
        .reshape(atom_count, K_WIN)
    )
    grad_pair_local = jnp.einsum(
        "acj,aj->c", pair_feats, bias_grad, preferred_element_type=jnp.float32
    )[:, None]
    factor = (samples * atom_count * slab_total) ** (-0.5)
    grad_proj_total, grad_out_total, grad_pair_total, grad_tok_total = lax.psum(
        (grad_proj_local, grad_out_local, grad_pair_local, grad_tok_local), "slab"
    )
    return (
        tok_act,
        grad_proj_total * factor,
        grad_out_total * factor,
        grad_pair_total * factor,
        grad_tok_total * factor,
    )


def solution(mesh):
    return jax.shard_map(
        on_device,
        mesh=mesh,
        in_specs=(
            P(None, "slab", None),
            P("slab", None, None),
            P("slab"),
            P(None, None, "head"),
            P("head", None),
            P(None, "head"),
            P(None, "head"),
            P(None, "slab", "head"),
        ),
        out_specs=(
            P(None, "slab", "head"),
            P(None, None, "head"),
            P("head", None),
            P(None, "head"),
            P(None, "head"),
        ),
        check_vma=False,
    )
```

profile of v0, /device:TPU:0, one launch (start us, length us, event | category | flops | bytes accessed | tf_op | source)
XLA Modules:
  0.0 244.7 jit_solution(9373553838993672769)
XLA Ops:
  7.2 1.2 convert_reduce_fusion.1
  8.5 1.3 fusion.14
  9.9 1.5 fusion.76
  11.4 4.9 %collective-permute-start = (bf16[2,2,48,32]{2,3,0,1:T(8,128)(2,1)S(1)}, bf16[2,2,48,32]{2,3,0,1:T(8,128)(2,1)S(1)}, u32[]{:S(2)}, u32[]{:S(2)}) collective-permute-start(bf16[2,2,48,32]{2,3,0,1:T(8,128)(2,1)S(1)} %get-tuple-element.19), channel_id=1, source_target_pairs={{0,4},{4,8},{8,12},{12,16},{16,20},{20,24},{24,28},{1,5},{5,9},{9,... | collective-permute-start | bytes 36872 | tf_op jit(solution)/shard_map/ppermute | solution.py:20
  16.3 1.3 collective-permute-start.1
  17.6 0.7 slice.103
  18.3 0.9 convert_reduce_fusion.2
  19.2 0.5 broadcast_maximum_fusion
  20.0 0.4 fusion.64
  20.4 5.6 %all-gather = bf16[128,128]{1,0:T(8,128)(2,1)} all-gather(bf16[32,128]{1,0:T(8,128)(2,1)S(1)} %copy-done.20), channel_id=2, replica_groups=mesh['slab'=8,'head'=4] {'head'}, dimensions={0}, use_global_device_ids=true | all-gather | bytes 40960 | tf_op jit(solution)/shard_map/all_gather | solution.py:114
  26.1 0.6 copy-done.17
  26.7 1.7 fusion.37
  28.4 1.2 reshape.129
  29.7 0.9 copy.25
  30.6 0.3 reshape.130
  30.9 0.9 copy.26
  31.8 0.3 reshape.132
  32.1 0.9 copy.28
  33.0 0.3 reshape.131
  33.5 2.0 pad_maximum_fusion.1
  35.5 0.3 fusion.5
  35.8 0.8 copy-done.6
  36.6 1.0 fusion.77
  37.6 3.8 %fusion.29 = f32[2,16,32,32]{3,2,1,0:T(8,128)} fusion(bf16[2,2,16,128,32]{3,4,2,1,0:T(8,128)(2,1)S(1)} %pad_maximum_fusion.1, f32[2,16,32]{2,1,0:T(8,128)S(1)} %get-tuple-element.33, f32[2,16,32,128]{3,2,1,0:T(8,128)} %copy-done.6), kind=kOutput, calls=%fused_computation.63 | convolution fusion | flops 8782975 | bytes 1458176 | tf_op jit(solution)/shard_map/sbqk,sbkd->sbqd/dot_general | solution.py:103
  41.5 1.9 copy.48
  43.4 1.3 copy.47
  44.6 1.0 multiply_convert_fusion.3
  45.6 5.8 %all_gather.6 = bf16[4,2,512,32]{2,3,0,1:T(8,128)(2,1)S(1)} all-gather(bf16[1,2,512,32]{2,3,0,1:T(8,128)(2,1)S(1)} %multiply_convert_fusion.3), channel_id=1, replica_groups=mesh['slab'=8,'head'=4] {'head'}, dimensions={0}, use_global_device_ids=true | all-gather | bytes 327680 | tf_op jit(solution)/shard_map/all_gather | solution.py:113
  51.4 0.5 convolution_convert_fusion
  52.1 0.3 fusion.51
  52.4 1.0 fusion.8
  53.4 0.5 fusion.3
  53.9 0.3 copy-done.12
  54.2 1.1 convolution_convert_fusion.1
  55.3 0.2 all-reduce.13.cloned.1.call-start
  55.5 0.9 convolution_bitcast_fusion.4
  56.4 34.3 %all-reduce.11.cloned.1.call-done = bf16[2,512,128]{2,1,0:T(8,128)(2,1)} async-done(((bf16[2,512,128]{2,1,0:T(8,128)(2,1)}), bf16[2,512,128]{2,1,0:T(8,128)(2,1)}) %all-reduce.11.cloned.1.call-update) | async-done | bytes 262160 | tf_op jit(solution)/shard_map/psum | solution.py:137
  90.7 1.9 fusion.42
  92.8 3.8 %convolution_bitcast_fusion.1 = f32[1,2,16,128,32]{3,4,2,1,0:T(8,128)} fusion(bf16[2,16,32,32]{2,1,3,0:T(8,128)(2,1)S(1)} %reshape.135, f32[2,16,32]{2,1,0:T(8,128)S(1)} %get-tuple-element.33, f32[2,16,32,128]{3,2,1,0:T(8,128)} %copy-done.6), kind=kOutput, calls=%fused_computation.14 | convolution fusion | flops 8782975 | bytes 1118208 | tf_op jit(solution)/shard_map/sbqk,sbqd->sbkd/dot_general | solution.py:165
  96.6 1.6 multiply_reduce_fusion
  98.3 0.3 fusion.71
  98.6 1.0 fusion.6
  99.6 0.2 convolution_bitcast_fusion.2
  99.8 1.0 convolution_bitcast_fusion.7
  100.8 2.2 fusion.10
  103.0 1.6 copy.35
  104.6 2.3 reshape.136
  106.9 2.8 %copy.36 = f32[2,2,16,32,32]{3,2,4,1,0:T(8,128)} copy(f32[2,2,16,32,32]{3,4,2,1,0:T(8,128)} %get-tuple-element.14) | data formatting | bytes 524288 | tf_op jit(solution)/shard_map/slice | solution.py:49
  109.7 2.3 reshape.137
  112.1 2.8 %copy.38 = f32[2,2,16,32,32]{3,2,4,1,0:T(8,128)} copy(f32[2,2,16,32,32]{3,4,2,1,0:T(8,128)} %get-tuple-element.15) | data formatting | bytes 524288 | tf_op jit(solution)/shard_map/slice | solution.py:49
  114.9 2.3 reshape.139
  117.2 1.6 copy.37
  118.8 1.7 reshape.138
  120.4 1.5 fusion.72
  122.0 3.4 %collective-permute-start.2 = (bf16[2,2,48,32]{2,3,1,0:T(8,128)(2,1)S(1)}, bf16[2,2,48,32]{2,3,1,0:T(8,128)(2,1)S(1)}, u32[]{:S(2)}, u32[]{:S(2)}) collective-permute-start(bf16[2,2,48,32]{2,3,1,0:T(8,128)(2,1)S(1)} %get-tuple-element.21), channel_id=1, source_target_pairs={{0,4},{4,8},{8,12},{12,16},{16,20},{20,24},{24,28},{1,5},{5,9},{9,... | collective-permute-start | bytes 36872 | tf_op jit(solution)/shard_map/ppermute | solution.py:20
  125.4 1.3 collective-permute-start.3
  126.7 1.2 convolution_bitcast_fusion.6
  127.9 38.2 %all-reduce.6 = (f32[32,128]{1,0:T(8,128)S(1)}, f32[16,1]{0,1:T(1,128)S(1)}) all-reduce(f32[32,128]{1,0:T(8,128)S(1)} %convolution_bitcast_fusion.6, f32[16,1]{0,1:T(1,128)S(1)} %convolution_bitcast_fusion.7), channel_id=1, replica_groups=mesh['slab'=8,'head'=4] {'slab'}, use_global_device_ids=true, to_apply=%region_9.10 | all-reduce | flops 4112 | bytes 32896 | tf_op jit(solution)/shard_map/psum | solution.py:195
  166.1 0.6 broadcast_multiply_fusion.2
  167.3 1.1 convolution_bitcast_fusion.5
  168.4 0.5 broadcast_multiply_fusion.4
  168.9 66.0 %all-reduce.13.cloned.1.call-done = (f32[4,128,32]{1,2,0:T(8,128)}, f32[128,192]{0,1:T(8,128)}) async-done(((f32[4,128,32]{1,2,0:T(8,128)}, f32[128,192]{0,1:T(8,128)}), (f32[4,128,32]{1,2,0:T(8,128)}, f32[128,192]{0,1:T(8,128)})) %all-reduce.13.cloned.1.call-update) | async-done | bytes 163856 | tf_op jit(solution)/shard_map/psum | solution.py:195
  234.9 1.5 broadcast_multiply_fusion.1
  236.4 1.5 broadcast_multiply_fusion
  (76 shorter events, 1.6 us)
Async XLA Ops:
  7.2 12.8 %copy-start = (bf16[512,16,128]{2,1,0:T(8,128)(2,1)S(1)}, bf16[512,16,128]{2,1,0:T(8,128)(2,1)}, u32[]{:S(2)}) copy-start(bf16[512,16,128]{2,1,0:T(8,128)(2,1)} %param.9) | copy-start | bytes 6291460
  7.2 12.8 %copy-start.22 = (bf16[16,1]{0,1:T(2,128)(2,1)S(1)}, bf16[16,1]{0,1:T(2,128)(2,1)}, u32[]{:S(2)}) copy-start(bf16[16,1]{0,1:T(2,128)(2,1)} %param.13) | copy-start | bytes 100
  7.2 83.5 %all-reduce.11.cloned.1.call-start = ((), (), s32[]{:S(2)}) async-start(), calls=%async_computation | async-start | bytes 524288 | tf_op jit(solution)/shard_map/psum | solution.py:137
  8.5 1.3 copy-start.15
  9.8 7.8 %copy-start.18 = (f32[2,512]{1,0:T(2,128)}, f32[2,512]{1,0:T(2,128)S(1)}, u32[]{:S(2)}) copy-start(f32[2,512]{1,0:T(2,128)S(1)} %add_rsqrt_fusion) | copy-start | bytes 12292
  9.8 10.6 %copy-start.20 = (bf16[32,128]{1,0:T(8,128)(2,1)S(1)}, bf16[32,128]{1,0:T(8,128)(2,1)}, u32[]{:S(2)}) copy-start(bf16[32,128]{1,0:T(8,128)(2,1)} %param.12) | copy-start | bytes 24580
  11.3 17.1 %copy-start.7 = (f32[4,2,512,32]{2,3,0,1:T(8,128)}, f32[4,2,512,32]{2,3,0,1:T(8,128)S(1)}, u32[]{:S(2)}) copy-start(f32[4,2,512,32]{2,3,0,1:T(8,128)S(1)} %get-tuple-element.32) | copy-start | bytes 1572868
  11.4 14.6 %collective-permute-start = (bf16[2,2,48,32]{2,3,0,1:T(8,128)(2,1)S(1)}, bf16[2,2,48,32]{2,3,0,1:T(8,128)(2,1)S(1)}, u32[]{:S(2)}, u32[]{:S(2)}) collective-permute-start(bf16[2,2,48,32]{2,3,0,1:T(8,128)(2,1)S(1)} %get-tuple-element.19), channel_id=1, source_target_pairs={{0,4},{4,8},{8,12},{12,16},{16,20},{20,24},{24,28},{1,5},{5,9},{9,... | collective-permute-start | bytes 36872 | tf_op jit(solution)/shard_map/ppermute | solution.py:20
  16.3 10.4 %collective-permute-start.1 = (bf16[2,2,48,32]{2,3,0,1:T(8,128)(2,1)S(1)}, bf16[2,2,48,32]{2,3,0,1:T(8,128)(2,1)}, u32[]{:S(2)}, u32[]{:S(2)}) collective-permute-start(bf16[2,2,48,32]{2,3,0,1:T(8,128)(2,1)S(1)} %get-tuple-element.20), channel_id=1, source_target_pairs={{4,0},{8,4},{12,8},{16,12},{20,16},{24,20},{28,24},{5,1},{9,5},{13... | collective-permute-start | bytes 36872 | tf_op jit(solution)/shard_map/ppermute | solution.py:22
  18.3 1.5 copy-start.23
  20.0 6.7 %copy-start.10 = (bf16[2,2,512,32]{2,3,0,1:T(8,128)(2,1)S(1)}, bf16[2,2,512,32]{2,3,0,1:T(8,128)(2,1)}, u32[]{:S(2)}) copy-start(bf16[2,2,512,32]{2,3,0,1:T(8,128)(2,1)} %slice.103) | copy-start | bytes 393220
  26.1 0.6 copy-start.17
  35.5 6.0 %copy-start.2 = (bf16[2,2,16,128,32]{3,4,2,1,0:T(8,128)(2,1)}, bf16[2,2,16,128,32]{3,4,2,1,0:T(8,128)(2,1)S(1)}, u32[]{:S(2)}) copy-start(bf16[2,2,16,128,32]{3,4,2,1,0:T(8,128)(2,1)S(1)} %pad_maximum_fusion.1) | copy-start | bytes 1572868
  35.8 0.8 copy-start.6
  37.6 13.8 %copy-start.14 = (bf16[128,128]{1,0:T(8,128)(2,1)S(1)}, bf16[128,128]{1,0:T(8,128)(2,1)}, u32[]{:S(2)}) copy-start(bf16[128,128]{1,0:T(8,128)(2,1)} %all-gather) | copy-start | bytes 98308
  43.4 8.8 %copy-start.1 = (bf16[2,512,128]{2,1,0:T(8,128)(2,1)S(1)}, bf16[2,512,128]{2,1,0:T(8,128)(2,1)}, u32[]{:S(2)}) copy-start(bf16[2,512,128]{2,1,0:T(8,128)(2,1)} %param.8) | copy-start | bytes 786436
  43.4 8.8 %copy-start.11 = (bf16[128,192]{0,1:T(8,128)(2,1)S(1)}, bf16[128,192]{0,1:T(8,128)(2,1)}, u32[]{:S(2)}) copy-start(bf16[128,192]{0,1:T(8,128)(2,1)} %param.14) | copy-start | bytes 147460
  51.4 1.0 copy-start.21
  51.4 1.0 copy-start.24
  51.4 1.0 copy-start.26
  52.4 1.0 copy-start.25
  53.4 0.8 copy-start.12
  55.3 179.6 %all-reduce.13.cloned.1.call-start = ((), (), s32[]{:S(2)}) async-start(), calls=%async_computation.1 | async-start | bytes 327680 | tf_op jit(solution)/shard_map/psum | solution.py:195
  56.4 40.2 %copy-start.3 = (bf16[2,2,16,128,32]{3,4,2,1,0:T(8,128)(2,1)S(1)}, bf16[2,2,16,128,32]{3,4,2,1,0:T(8,128)(2,1)}, u32[]{:S(2)}) copy-start(bf16[2,2,16,128,32]{3,4,2,1,0:T(8,128)(2,1)} %copy-done.2) | copy-start | bytes 1572868
  96.6 1.6 copy-start.5
  96.6 2.0 copy-start.4
  99.6 1.2 copy-start.9
  117.2 9.5 %copy-start.13 = (f32[2,512,32]{1,2,0:T(8,128)S(1)}, f32[2,512,32]{1,2,0:T(8,128)}, u32[]{:S(2)}) copy-start(f32[2,512,32]{1,2,0:T(8,128)} %copy.48) | copy-start | bytes 393220
  118.8 48.0 %copy-start.8 = (bf16[2,16,32,32]{3,2,1,0:T(8,128)(2,1)S(1)}, bf16[2,16,32,32]{3,2,1,0:T(8,128)(2,1)}, u32[]{:S(2)}) copy-start(bf16[2,16,32,32]{3,2,1,0:T(8,128)(2,1)} %fusion.6) | copy-start | bytes 196612
  120.4 46.8 %copy-start.16 = (f32[2,512]{1,0:T(2,128)S(1)}, f32[2,512]{1,0:T(2,128)}, u32[]{:S(2)}) copy-start(f32[2,512]{1,0:T(2,128)} %copy-done.15) | copy-start | bytes 12292
  120.4 46.8 %copy-start.19 = (f32[2,512]{1,0:T(2,128)S(1)}, f32[2,512]{1,0:T(2,128)}, u32[]{:S(2)}) copy-start(f32[2,512]{1,0:T(2,128)} %copy-done.18) | copy-start | bytes 12292
  120.4 46.8 %copy-start.27 = (bf16[1,2,512,32]{2,3,1,0:T(8,128)(2,1)S(1)}, bf16[1,2,512,32]{2,3,1,0:T(8,128)(2,1)}, u32[]{:S(2)}) copy-start(bf16[1,2,512,32]{2,3,1,0:T(8,128)(2,1)} %get-tuple-element.18) | copy-start | bytes 196612
  122.0 44.9 %collective-permute-start.2 = (bf16[2,2,48,32]{2,3,1,0:T(8,128)(2,1)S(1)}, bf16[2,2,48,32]{2,3,1,0:T(8,128)(2,1)S(1)}, u32[]{:S(2)}, u32[]{:S(2)}) collective-permute-start(bf16[2,2,48,32]{2,3,1,0:T(8,128)(2,1)S(1)} %get-tuple-element.21), channel_id=1, source_target_pairs={{0,4},{4,8},{8,12},{12,16},{16,20},{20,24},{24,28},{1,5},{5,9},{9,... | collective-permute-start | bytes 36872 | tf_op jit(solution)/shard_map/ppermute | solution.py:20
  125.4 41.5 %collective-permute-start.3 = (bf16[2,2,48,32]{2,3,1,0:T(8,128)(2,1)S(1)}, bf16[2,2,48,32]{2,3,1,0:T(8,128)(2,1)S(1)}, u32[]{:S(2)}, u32[]{:S(2)}) collective-permute-start(bf16[2,2,48,32]{2,3,1,0:T(8,128)(2,1)S(1)} %get-tuple-element.22), channel_id=1, source_target_pairs={{4,0},{8,4},{12,8},{16,12},{20,16},{24,20},{28,24},{5,1},{9,5},{13... | collective-permute-start | bytes 36872 | tf_op jit(solution)/shard_map/ppermute | solution.py:22
Sparse Core Ops, SparseCore 0:
  55.4 35.2 all-reduce.10
  168.5 66.3 all-reduce.12
where the time goes:
time: 246 us; the launch traced here: 245 us
  waiting for transfers between devices  100 us (41%)
  blocking collectives  49.7 us (20%)
  local copies, waits for them, and re-layouts  28.7 us (12%)
  matrix products  22 us (9%)
  other arithmetic  18.4 us (7%)
  between operations  14.5 us (6%)
  starting transfers between devices  11.1 us (5%)
    psum x1, waiting for transfers between devices, on_device(): lax.psum((grad_proj_local, grad_out_local, grad_pair_local, grad_tok_loca...  66 us
    psum x1, blocking collectives, on_device(): lax.psum((grad_proj_local, grad_out_local, grad_pair_local, grad_tok_loca...  38.2 us
    psum x1, waiting for transfers between devices, on_device(): mixed_grad = lax.psum(mixed_terms.astype(jnp.bfloat16), 'head')  34.3 us
    slice x4, local copies, waits for them, and re-layouts, key_unwindowed_rows(): windowed[..., Q_WIN * offset:Q_WIN * (offset + 1), :]  8.83 us
    reshape x4, local copies, waits for them, and re-layouts, key_unwindowed_rows(): windowed[..., Q_WIN * offset:Q_WIN * (offset + 1), :]  8.59 us
    ppermute x2, starting transfers between devices, extended_2(): lax.ppermute(tail, axis, [(i, (i + 1) % count) for i in range(ends)])  8.23 us
    all_gather x1, blocking collectives, on_device(): lax.all_gather(heads_out[None], 'head', axis=0, tiled=True)  5.85 us
    all_gather x1, blocking collectives, on_device(): lax.all_gather(w_out[None], 'head', axis=0, tiled=True)  5.64 us
  transfers between devices with their start and end apart: 6, of which 2 were waited for; matrix products, arithmetic and copies ran while one was open for 2% of the time, Pallas kernels for 0%

commit v1 on v0

--- a/solution.py
+++ b/solution.py
@@ -134,7 +134,7 @@
         "saw,sah->wh", mixed_half, act_grad, preferred_element_type=jnp.float32
     )
     mixed_terms = jnp.einsum("sah,wh->saw", act_grad, w_tok, preferred_element_type=jnp.float32)
-    mixed_grad = lax.psum(mixed_terms.astype(jnp.bfloat16), "head")
+    mixed_grad = jnp.sum(lax.all_gather(mixed_terms.astype(jnp.bfloat16), "head"), axis=0)
     out_grad = jnp.einsum("saw,dw->sad", mixed_grad, w_out, preferred_element_type=jnp.float32)
     grad_out_local = jnp.einsum(
         "sad,saw->dw", heads_out, mixed_grad, preferred_element_type=jnp.float32

time: 246 us -> 230 us (0.935)
  waiting for transfers between devices: 100 us -> 80.8 us
    psum x1 -> x0, waiting for transfers between devices: 34.3 us -> none  [on_device(): mixed_grad = lax.psum(mixed_terms.astype(jnp.bfloat16), 'head')]
    all_gather x0 -> x1, waiting for transfers between devices: none -> 14.7 us  [on_device(): lax.all_gather(mixed_terms.astype(jnp.bfloat16), 'head')]
  transfers between devices with their start and end apart: 6 -> 6, of which waited for: 2 -> 2; matrix products, arithmetic and copies ran while one was open for 2% -> 4% of each run, Pallas kernels for 0% -> 0%
where the time goes in v1:
time: 230 us; the launch traced here: 229 us
  waiting for transfers between devices  80.8 us (35%)
  blocking collectives  49.8 us (22%)
  local copies, waits for them, and re-layouts  29.8 us (13%)
  matrix products  23.6 us (10%)
  other arithmetic  19.8 us (9%)
  between operations  14.5 us (6%)
  starting transfers between devices  11.1 us (5%)
    psum x1, waiting for transfers between devices, on_device(): lax.psum((grad_proj_local, grad_out_local, grad_pair_local, grad_tok_loca...  66.1 us
    psum x1, blocking collectives, on_device(): lax.psum((grad_proj_local, grad_out_local, grad_pair_local, grad_tok_loca...  38.3 us
    all_gather x1, waiting for transfers between devices, on_device(): lax.all_gather(mixed_terms.astype(jnp.bfloat16), 'head')  14.7 us
    slice x4, local copies, waits for them, and re-layouts, key_unwindowed_rows(): windowed[..., Q_WIN * offset:Q_WIN * (offset + 1), :]  8.8 us
    reshape x4, local copies, waits for them, and re-layouts, key_unwindowed_rows(): windowed[..., Q_WIN * offset:Q_WIN * (offset + 1), :]  8.62 us
    ppermute x2, starting transfers between devices, extended_2(): lax.ppermute(tail, axis, [(i, (i + 1) % count) for i in range(ends)])  8.24 us
    all_gather x1, blocking collectives, on_device(): lax.all_gather(heads_out[None], 'head', axis=0, tiled=True)  5.85 us
    all_gather x1, blocking collectives, on_device(): lax.all_gather(w_out[None], 'head', axis=0, tiled=True)  5.64 us
  transfers between devices with their start and end apart: 6, of which 2 were waited for; matrix products, arithmetic and copies ran while one was open for 4% of the time, Pallas kernels for 0%

profile of v1, /device:TPU:0, one launch (start us, length us, event | category | flops | bytes accessed | tf_op | source)
XLA Modules:
  0.0 229.4 jit_solution(14599161264125893007)
XLA Ops:
  7.2 1.2 convert_reduce_fusion.1
  8.5 1.3 fusion.14
  9.9 1.5 fusion.76
  11.4 4.9 %collective-permute-start = (bf16[2,2,48,32]{2,3,0,1:T(8,128)(2,1)S(1)}, bf16[2,2,48,32]{2,3,0,1:T(8,128)(2,1)S(1)}, u32[]{:S(2)}, u32[]{:S(2)}) collective-permute-start(bf16[2,2,48,32]{2,3,0,1:T(8,128)(2,1)S(1)} %get-tuple-element.19), channel_id=1, source_target_pairs={{0,4},{4,8},{8,12},{12,16},{16,20},{20,24},{24,28},{1,5},{5,9},{9,... | collective-permute-start | bytes 36872 | tf_op jit(solution)/shard_map/ppermute | solution.py:20
  16.3 1.3 collective-permute-start.1
  17.6 0.7 slice.103
  18.3 0.9 convert_reduce_fusion.2
  19.2 0.5 broadcast_maximum_fusion
  20.0 0.4 fusion.64
  20.4 5.6 %all-gather = bf16[128,128]{1,0:T(8,128)(2,1)} all-gather(bf16[32,128]{1,0:T(8,128)(2,1)S(1)} %copy-done.22), channel_id=2, replica_groups=mesh['slab'=8,'head'=4] {'head'}, dimensions={0}, use_global_device_ids=true | all-gather | bytes 40960 | tf_op jit(solution)/shard_map/all_gather | solution.py:114
  26.1 0.6 copy-done.18
  26.7 1.7 fusion.37
  28.4 1.2 reshape.129
  29.7 1.0 copy.41
  30.6 0.3 reshape.130
  30.9 0.9 copy.42
  31.9 0.3 reshape.132
  32.1 0.9 copy.44
  33.1 0.3 reshape.131
  33.5 2.0 pad_maximum_fusion.1
  35.6 0.3 fusion.5
  35.9 0.8 copy-done.6
  36.7 1.0 fusion.77
  37.7 3.8 %fusion.29 = f32[2,16,32,32]{3,2,1,0:T(8,128)} fusion(bf16[2,2,16,128,32]{3,4,2,1,0:T(8,128)(2,1)S(1)} %pad_maximum_fusion.1, f32[2,16,32]{2,1,0:T(8,128)S(1)} %get-tuple-element.33, f32[2,16,32,128]{3,2,1,0:T(8,128)} %copy-done.6), kind=kOutput, calls=%fused_computation.63 | convolution fusion | flops 8782975 | bytes 1458176 | tf_op jit(solution)/shard_map/sbqk,sbkd->sbqd/dot_general | solution.py:103
  41.5 1.3 copy.63
  42.8 1.0 multiply_convert_fusion.3
  43.7 5.9 %all_gather.12 = bf16[4,2,512,32]{2,3,0,1:T(8,128)(2,1)S(1)} all-gather(bf16[1,2,512,32]{2,3,0,1:T(8,128)(2,1)S(1)} %multiply_convert_fusion.3), channel_id=1, replica_groups=mesh['slab'=8,'head'=4] {'head'}, dimensions={0}, use_global_device_ids=true | all-gather | bytes 327680 | tf_op jit(solution)/shard_map/all_gather | solution.py:113
  49.6 0.5 convolution_convert_fusion
  50.3 0.3 fusion.51
  50.6 0.5 fusion.3
  51.1 0.4 copy-done.9
  51.6 1.1 convolution_convert_fusion.1
  52.9 1.9 copy.64
  54.7 0.9 convolution_bitcast_fusion.4
  55.6 2.1 fusion.8
  57.8 14.7 %all-gather.4.cloned.1.call-done = bf16[8,512,128]{2,1,0:T(8,128)(2,1)} async-done(((bf16[2,512,128]{2,1,0:T(8,128)(2,1)}), bf16[8,512,128]{2,1,0:T(8,128)(2,1)}) %all-gather.4.cloned.1.call-update) | async-done | bytes 1048592 | tf_op jit(solution)/shard_map/all_gather | solution.py:137
  72.5 1.5 reduce_sum.83
  74.0 1.7 convolution_bitcast_fusion.6
  75.7 1.8 fusion.42
  77.5 1.0 reshape.135
  78.5 3.8 %convolution_bitcast_fusion.1 = f32[1,2,16,128,32]{3,4,2,1,0:T(8,128)} fusion(bf16[2,16,32,32]{2,1,3,0:T(8,128)(2,1)S(1)} %reshape.135, f32[2,16,32]{2,1,0:T(8,128)S(1)} %get-tuple-element.33, f32[2,16,32,128]{3,2,1,0:T(8,128)} %copy-done.6), kind=kOutput, calls=%fused_computation.14 | convolution fusion | flops 8782975 | bytes 1118208 | tf_op jit(solution)/shard_map/sbqk,sbqd->sbkd/dot_general | solution.py:165
  82.4 1.6 multiply_reduce_fusion
  84.0 0.3 fusion.71
  84.3 1.0 fusion.6
  85.5 1.0 convolution_bitcast_fusion.7
  86.5 2.3 fusion.10
  88.7 1.6 copy.51
  90.3 2.3 %reshape.136 = f32[2,2,512,32]{2,3,1,0:T(8,128)} reshape(f32[2,2,16,32,32]{3,2,4,1,0:T(8,128)} %copy.51) | data formatting | bytes 524288 | tf_op jit(solution)/shard_map/reshape | solution.py:49
  92.6 2.8 %copy.52 = f32[2,2,16,32,32]{3,2,4,1,0:T(8,128)} copy(f32[2,2,16,32,32]{3,4,2,1,0:T(8,128)} %get-tuple-element.14) | data formatting | bytes 524288 | tf_op jit(solution)/shard_map/slice | solution.py:49
  95.4 2.3 %reshape.137 = f32[2,2,512,32]{2,3,1,0:T(8,128)} reshape(f32[2,2,16,32,32]{3,2,4,1,0:T(8,128)} %copy.52) | data formatting | bytes 524288 | tf_op jit(solution)/shard_map/reshape | solution.py:49
  97.8 2.8 %copy.54 = f32[2,2,16,32,32]{3,2,4,1,0:T(8,128)} copy(f32[2,2,16,32,32]{3,4,2,1,0:T(8,128)} %get-tuple-element.15) | data formatting | bytes 524288 | tf_op jit(solution)/shard_map/slice | solution.py:49
  100.6 2.3 %reshape.139 = f32[2,2,512,32]{2,3,1,0:T(8,128)} reshape(f32[2,2,16,32,32]{3,2,4,1,0:T(8,128)} %copy.54) | data formatting | bytes 524288 | tf_op jit(solution)/shard_map/reshape | solution.py:49
  102.9 1.6 copy.53
  104.5 1.7 reshape.138
  106.2 1.4 fusion.72
  107.7 3.4 %collective-permute-start.2 = (bf16[2,2,48,32]{2,3,1,0:T(8,128)(2,1)S(1)}, bf16[2,2,48,32]{2,3,1,0:T(8,128)(2,1)S(1)}, u32[]{:S(2)}, u32[]{:S(2)}) collective-permute-start(bf16[2,2,48,32]{2,3,1,0:T(8,128)(2,1)S(1)} %get-tuple-element.21), channel_id=1, source_target_pairs={{0,4},{4,8},{8,12},{12,16},{16,20},{20,24},{24,28},{1,5},{5,9},{9,... | collective-permute-start | bytes 36872 | tf_op jit(solution)/shard_map/ppermute | solution.py:20
  111.1 1.3 collective-permute-start.3
  112.4 38.3 %all-reduce.6 = (f32[32,128]{1,0:T(8,128)S(1)}, f32[16,1]{0,1:T(1,128)S(1)}) all-reduce(f32[32,128]{1,0:T(8,128)S(1)} %copy-done.21, f32[16,1]{0,1:T(1,128)S(1)} %convolution_bitcast_fusion.7), channel_id=1, replica_groups=mesh['slab'=8,'head'=4] {'slab'}, use_global_device_ids=true, to_apply=%region_9.10 | all-reduce | flops 4112 | bytes 32896 | tf_op jit(solution)/shard_map/psum | solution.py:195
  150.7 0.6 broadcast_multiply_fusion.2
  151.8 1.1 convolution_bitcast_fusion.5
  153.0 0.5 broadcast_multiply_fusion.4
  153.5 66.1 %all-reduce.10.cloned.1.call-done = (f32[4,128,32]{1,2,0:T(8,128)}, f32[128,192]{0,1:T(8,128)}) async-done(((f32[4,128,32]{1,2,0:T(8,128)}, f32[128,192]{0,1:T(8,128)}), (f32[4,128,32]{1,2,0:T(8,128)}, f32[128,192]{0,1:T(8,128)})) %all-reduce.10.cloned.1.call-update) | async-done | bytes 163856 | tf_op jit(solution)/shard_map/psum | solution.py:195
  219.6 1.5 broadcast_multiply_fusion.1
  221.0 1.5 broadcast_multiply_fusion
  (81 shorter events, 1.8 us)
Async XLA Ops:
  7.2 12.8 %copy-start = (bf16[512,16,128]{2,1,0:T(8,128)(2,1)S(1)}, bf16[512,16,128]{2,1,0:T(8,128)(2,1)}, u32[]{:S(2)}) copy-start(bf16[512,16,128]{2,1,0:T(8,128)(2,1)} %param.9) | copy-start | bytes 6291460
  7.2 12.8 %copy-start.24 = (bf16[16,1]{0,1:T(2,128)(2,1)S(1)}, bf16[16,1]{0,1:T(2,128)(2,1)}, u32[]{:S(2)}) copy-start(bf16[16,1]{0,1:T(2,128)(2,1)} %param.13) | copy-start | bytes 100
  7.2 65.3 %all-gather.4.cloned.1.call-start = ((), (), s32[]{:S(2)}) async-start(), calls=%async_computation | async-start | bytes 1310720 | tf_op jit(solution)/shard_map/all_gather | solution.py:137
  8.5 1.3 copy-start.16
  9.8 7.8 %copy-start.19 = (f32[2,512]{1,0:T(2,128)}, f32[2,512]{1,0:T(2,128)S(1)}, u32[]{:S(2)}) copy-start(f32[2,512]{1,0:T(2,128)S(1)} %add_rsqrt_fusion) | copy-start | bytes 12292
  9.8 10.6 %copy-start.22 = (bf16[32,128]{1,0:T(8,128)(2,1)S(1)}, bf16[32,128]{1,0:T(8,128)(2,1)}, u32[]{:S(2)}) copy-start(bf16[32,128]{1,0:T(8,128)(2,1)} %param.12) | copy-start | bytes 24580
  11.3 17.1 %copy-start.7 = (f32[4,2,512,32]{2,3,0,1:T(8,128)}, f32[4,2,512,32]{2,3,0,1:T(8,128)S(1)}, u32[]{:S(2)}) copy-start(f32[4,2,512,32]{2,3,0,1:T(8,128)S(1)} %get-tuple-element.32) | copy-start | bytes 1572868
  11.4 14.7 %collective-permute-start = (bf16[2,2,48,32]{2,3,0,1:T(8,128)(2,1)S(1)}, bf16[2,2,48,32]{2,3,0,1:T(8,128)(2,1)S(1)}, u32[]{:S(2)}, u32[]{:S(2)}) collective-permute-start(bf16[2,2,48,32]{2,3,0,1:T(8,128)(2,1)S(1)} %get-tuple-element.19), channel_id=1, source_target_pairs={{0,4},{4,8},{8,12},{12,16},{16,20},{20,24},{24,28},{1,5},{5,9},{9,... | collective-permute-start | bytes 36872 | tf_op jit(solution)/shard_map/ppermute | solution.py:20
  16.3 10.4 %collective-permute-start.1 = (bf16[2,2,48,32]{2,3,0,1:T(8,128)(2,1)S(1)}, bf16[2,2,48,32]{2,3,0,1:T(8,128)(2,1)}, u32[]{:S(2)}, u32[]{:S(2)}) collective-permute-start(bf16[2,2,48,32]{2,3,0,1:T(8,128)(2,1)S(1)} %get-tuple-element.20), channel_id=1, source_target_pairs={{4,0},{8,4},{12,8},{16,12},{20,16},{24,20},{28,24},{5,1},{9,5},{13... | collective-permute-start | bytes 36872 | tf_op jit(solution)/shard_map/ppermute | solution.py:22
  18.3 1.5 copy-start.25
  20.0 6.7 %copy-start.11 = (bf16[2,2,512,32]{2,3,0,1:T(8,128)(2,1)S(1)}, bf16[2,2,512,32]{2,3,0,1:T(8,128)(2,1)}, u32[]{:S(2)}) copy-start(bf16[2,2,512,32]{2,3,0,1:T(8,128)(2,1)} %slice.103) | copy-start | bytes 393220
  26.1 0.6 copy-start.18
  35.5 6.0 %copy-start.2 = (bf16[2,2,16,128,32]{3,4,2,1,0:T(8,128)(2,1)}, bf16[2,2,16,128,32]{3,4,2,1,0:T(8,128)(2,1)S(1)}, u32[]{:S(2)}) copy-start(bf16[2,2,16,128,32]{3,4,2,1,0:T(8,128)(2,1)S(1)} %pad_maximum_fusion.1) | copy-start | bytes 1572868
  35.8 0.8 copy-start.6
  37.7 11.9 %copy-start.15 = (bf16[128,128]{1,0:T(8,128)(2,1)S(1)}, bf16[128,128]{1,0:T(8,128)(2,1)}, u32[]{:S(2)}) copy-start(bf16[128,128]{1,0:T(8,128)(2,1)} %all-gather) | copy-start | bytes 98308
  41.5 8.8 %copy-start.1 = (bf16[2,512,128]{2,1,0:T(8,128)(2,1)S(1)}, bf16[2,512,128]{2,1,0:T(8,128)(2,1)}, u32[]{:S(2)}) copy-start(bf16[2,512,128]{2,1,0:T(8,128)(2,1)} %param.8) | copy-start | bytes 786436
  41.5 8.8 %copy-start.12 = (bf16[128,192]{0,1:T(8,128)(2,1)S(1)}, bf16[128,192]{0,1:T(8,128)(2,1)}, u32[]{:S(2)}) copy-start(bf16[128,192]{0,1:T(8,128)(2,1)} %param.14) | copy-start | bytes 147460
  49.6 1.0 copy-start.23
  49.6 1.0 copy-start.26
  49.6 1.0 copy-start.27
  49.6 1.0 copy-start.28
  50.6 0.9 copy-start.9
  50.6 0.9 copy-start.13
  52.6 166.9 %all-reduce.10.cloned.1.call-start = ((), (), s32[]{:S(2)}) async-start(), calls=%async_computation.1 | async-start | bytes 327680 | tf_op jit(solution)/shard_map/psum | solution.py:195
  55.6 18.3 %copy-start.14 = (f32[2,512,32]{1,2,0:T(8,128)S(1)}, f32[2,512,32]{1,2,0:T(8,128)}, u32[]{:S(2)}) copy-start(f32[2,512,32]{1,2,0:T(8,128)} %copy.64) | copy-start | bytes 393220
  74.0 8.4 %copy-start.3 = (bf16[2,2,16,128,32]{3,4,2,1,0:T(8,128)(2,1)S(1)}, bf16[2,2,16,128,32]{3,4,2,1,0:T(8,128)(2,1)}, u32[]{:S(2)}) copy-start(bf16[2,2,16,128,32]{3,4,2,1,0:T(8,128)(2,1)} %copy-done.2) | copy-start | bytes 1572868
  82.4 1.6 copy-start.5
  82.4 2.0 copy-start.4
  85.3 1.2 copy-start.10
  102.9 9.5 %copy-start.21 = (f32[32,128]{1,0:T(8,128)S(1)}, f32[32,128]{1,0:T(8,128)}, u32[]{:S(2)}) copy-start(f32[32,128]{1,0:T(8,128)} %convolution_bitcast_fusion.6) | copy-start | bytes 49156
  104.5 46.8 %copy-start.8 = (bf16[2,16,32,32]{3,2,1,0:T(8,128)(2,1)S(1)}, bf16[2,16,32,32]{3,2,1,0:T(8,128)(2,1)}, u32[]{:S(2)}) copy-start(bf16[2,16,32,32]{3,2,1,0:T(8,128)(2,1)} %fusion.6) | copy-start | bytes 196612
  104.5 47.3 %copy-start.17 = (f32[2,512]{1,0:T(2,128)S(1)}, f32[2,512]{1,0:T(2,128)}, u32[]{:S(2)}) copy-start(f32[2,512]{1,0:T(2,128)} %copy-done.16) | copy-start | bytes 12292
  104.5 47.3 %copy-start.20 = (f32[2,512]{1,0:T(2,128)S(1)}, f32[2,512]{1,0:T(2,128)}, u32[]{:S(2)}) copy-start(f32[2,512]{1,0:T(2,128)} %copy-done.19) | copy-start | bytes 12292
  104.5 47.3 %copy-start.29 = (bf16[1,2,512,32]{2,3,1,0:T(8,128)(2,1)S(1)}, bf16[1,2,512,32]{2,3,1,0:T(8,128)(2,1)}, u32[]{:S(2)}) copy-start(bf16[1,2,512,32]{2,3,1,0:T(8,128)(2,1)} %get-tuple-element.18) | copy-start | bytes 196612
  107.7 43.7 %collective-permute-start.2 = (bf16[2,2,48,32]{2,3,1,0:T(8,128)(2,1)S(1)}, bf16[2,2,48,32]{2,3,1,0:T(8,128)(2,1)S(1)}, u32[]{:S(2)}, u32[]{:S(2)}) collective-permute-start(bf16[2,2,48,32]{2,3,1,0:T(8,128)(2,1)S(1)} %get-tuple-element.21), channel_id=1, source_target_pairs={{0,4},{4,8},{8,12},{12,16},{16,20},{20,24},{24,28},{1,5},{5,9},{9,... | collective-permute-start | bytes 36872 | tf_op jit(solution)/shard_map/ppermute | solution.py:20
  111.1 40.3 %collective-permute-start.3 = (bf16[2,2,48,32]{2,3,1,0:T(8,128)(2,1)S(1)}, bf16[2,2,48,32]{2,3,1,0:T(8,128)(2,1)S(1)}, u32[]{:S(2)}, u32[]{:S(2)}) collective-permute-start(bf16[2,2,48,32]{2,3,1,0:T(8,128)(2,1)S(1)} %get-tuple-element.22), channel_id=1, source_target_pairs={{4,0},{8,4},{12,8},{16,12},{20,16},{24,20},{28,24},{5,1},{9,5},{13... | collective-permute-start | bytes 36872 | tf_op jit(solution)/shard_map/ppermute | solution.py:22
Sparse Core Ops, SparseCore 0:
  52.8 19.6 all-gather.3
  153.1 66.4 all-reduce.9
